TPU v7x, 32 devices: a whole 2x2x4 slice. The times are simulated.
32 devices in a mesh: row: 4 (over y, x), col: 8 (over z, core).
Axes of the slice: x: 2, y: 2, z: 4, core: 2. Of those that a mesh axis runs over, the one named last changes fastest.
Arguments:
- schur: float32 [8192, 8192], P('row', 'col'), may hold values from -6 to 6
- panel_raw: bfloat16 [8192, 1024], P('col', 'row'), may hold values from -0.59765625 to 0.59765625
- diag_inverse: bfloat16 [1024, 1024], replicated, may hold values from -1 to 2, as said below
- perm: int32 [64], replicated, may hold values from 0 to 63, as said below
- pattern: int32 [64, 64], P('row', 'col'), may hold values 0 or 1
Outputs:
- schur_out: float32 [8192, 8192], P('row', 'col')
Inputs may be any that keep to these rules, and one draw needn't show every extreme that they name: diag_inverse is lower triangular with diagonal entries between 0.5 and 2. perm names every block row once. Holder h holds the owner-order blocks h * 8 to (h + 1) * 8 - 1; a column group is a run of 8 consecutive global block rows starting at a multiple of it. The blocks of one holder fall into the column groups as evenly as possible: at most 1 into one group, and exactly 1 into some group.
All inputs are finite; a program needn't handle non-finite values. No bound on the sum of `pattern` on one device may be relied on, other than what follows from the above.
Results may differ from a plain program's by a relative error of at most 0.007.
Values may be sent and summed in bfloat16 or wider, within the bound.
A program may use at most 192 MiB of HBM per device.

v0:
```python
import jax
import jax.numpy as jnp
from jax import lax
from jax.sharding import PartitionSpec as P

BLK = 128


def times_inverse(left, right):
    return lax.dot_general(
        left, right, (((1,), (1,)), ((), ())), preferred_element_type=jnp.float32
    )


def local(schur, panel_raw, diag_inverse, perm, pattern):
    row_count_axis = lax.axis_size("row")
    col_count_axis = lax.axis_size("col")
    row_index = lax.axis_index("row")
    col_index = lax.axis_index("col")
    owned_rows = panel_raw.shape[0]
    share_rows = owned_rows // row_count_axis
    blocks = perm.shape[0]
    position = jnp.zeros((blocks,), jnp.int32).at[perm].set(jnp.arange(blocks, dtype=jnp.int32))
    local_rows = schur.shape[0]
    local_cols = schur.shape[1]
    row_ids = row_index * local_rows + jnp.arange(local_rows, dtype=jnp.int32)
    col_ids = col_index * local_cols + jnp.arange(local_cols, dtype=jnp.int32)

    def owner_row(global_ids):
        return position[global_ids // BLK] * BLK + global_ids % BLK

    owner_of_rows = owner_row(row_ids)
    owner_of_cols = owner_row(col_ids)
    inv_cols = panel_raw.shape[1]
    inv_part = lax.dynamic_slice_in_dim(diag_inverse, row_index * inv_cols, inv_cols, 1)
    own_block = lax.psum_scatter(
        times_inverse(panel_raw, inv_part).astype(jnp.bfloat16),
        "row",
        scatter_dimension=0,
        tiled=True,
    ).astype(jnp.float32)
    own_block = own_block.astype(jnp.bfloat16)
    all_blocks = lax.all_gather(own_block, ("row", "col"), axis=0, tiled=True)

    def located(owner_ids):
        source_col = owner_ids // owned_rows
        source_row = owner_ids % owned_rows // share_rows
        return (source_row * col_count_axis + source_col) * share_rows + owner_ids % share_rows

    rows_panel = jnp.take(all_blocks, located(owner_of_rows), axis=0)
    cols_panel = jnp.take(all_blocks, located(owner_of_cols), axis=0)
    update = lax.dot_general(
        rows_panel, cols_panel, (((1,), (1,)), ((), ())), preferred_element_type=jnp.float32
    )
    block_rows = local_rows // BLK
    block_cols = local_cols // BLK
    masked = (
        update.reshape(block_rows, BLK, block_cols, BLK)
        * pattern.astype(jnp.float32)[:, None, :, None]
    )
    return schur - masked.reshape(local_rows, local_cols)


def solution(mesh):
    return jax.shard_map(
        local,
        mesh=mesh,
        in_specs=(P("row", "col"), P("col", "row"), P(), P(), P("row", "col")),
        out_specs=P("row", "col"),
        check_vma=False,
    )
```

profile of v0, /device:TPU:0, one launch (start us, length us, event | category | flops | bytes accessed | tf_op | source)
XLA Modules:
  0.0 267.7 jit_solution(14119523336762092420)
XLA Ops:
  6.6 1.6 copy-done
  8.1 3.1 %convert_bitcast_fusion = bf16[1024,1024]{0,1:T(8,128)(2,1)} fusion(bf16[1024,256]{1,0:T(8,128)(2,1)} %param.6, bf16[1024,1024]{1,0:T(8,128)(2,1)S(1)} %copy-done, s32[]{:T(128)S(6)} %select_n.248), kind=kOutput, calls=%fused_computation.9 | convolution fusion | flops 537919488 | bytes 3145732 | tf_op jit(solution)/shard_map/dot_general | solution.py:10
  11.3 38.0 %reduce-scatter.2.cloned.1.call-done = bf16[256,1024]{0,1:T(8,128)(2,1)} async-done(((bf16[1024,1024]{0,1:T(8,128)(2,1)}), bf16[256,1024]{0,1:T(8,128)(2,1)}) %reduce-scatter.2.cloned.1.call-update) | async-done | bytes 524304 | tf_op jit(solution)/shard_map/reduce_scatter | solution.py:36
  49.5 0.8 scatter_custom_fusion
  52.1 0.1 compare_reduce_fusion.46
  52.9 0.1 compare_reduce_fusion.28
  54.2 0.1 compare_reduce_fusion.16
  55.1 0.7 fusion.47
  55.8 4.5 %compare_select_fusion.17 = s32[1024,1]{0,1:T(1,128)S(1)} fusion(s32[]{:T(128)} %bitcast.57, s32[]{:T(128)} %bitcast.58, s32[]{:T(128)} %bitcast.59, s32[]{:T(128)} %bitcast.60, s32[]{:T(128)} %bitcast.61, s32[]{:T(128)} %bitcast.63, s32[]{:T(128)} %bitcast.62, s32[]{:T(128)S(6)} %mul.120), kind=kLoop, calls=%fused_computation.150 | loop fusion | flops 31744 | bytes 4128 | tf_op jit(solution)/shard_map/gather | solution.py:30
  60.3 0.7 fusion.45
  61.1 0.7 fusion.46
  61.8 0.7 fusion.44
  62.5 4.5 %compare_select_fusion.2 = s32[2048,1]{0,1:T(1,128)S(1)} fusion(s32[]{:T(128)} %bitcast.57, s32[]{:T(128)} %bitcast.58, s32[]{:T(128)} %bitcast.59, s32[]{:T(128)} %bitcast.60, s32[]{:T(128)} %bitcast.61, s32[]{:T(128)} %bitcast.63, s32[]{:T(128)} %bitcast.62, s32[]{:T(128)S(6)} %mul.112), kind=kLoop, calls=%fused_computation.72 | loop fusion | flops 63488 | bytes 8224 | tf_op jit(solution)/shard_map/gather | solution.py:30
  67.1 35.6 %compare_and_fusion.1 = (pred[1024]{0:T(1024)(128)(4,1)S(1)}, s32[1024]{0:T(1024)S(1)}) fusion(s32[]{:T(128)S(6)} %mul.120, pred[1024]{0:T(1024)(128)(4,1)S(1)} %get-tuple-element.129, pred[1024]{0:T(1024)(128)(4,1)S(1)} %get-tuple-element.130, pred[1024]{0:T(1024)(128)(4,1)S(1)} %get-tuple-element.131, pred[1024]{0:T(1024)(128)(4,1)S(1)} %get-tuple-element.132, ...), kind=kLoop, calls=%fused_computation.245 | loop fusion | flops 125952 | bytes 67816 | tf_op jit(solution)/shard_map/jit(_take)/and | solution.py:51
  102.8 35.7 %compare_and_fusion = (pred[2048]{0:T(1024)(128)(4,1)S(1)}, s32[2048]{0:T(1024)S(1)}) fusion(s32[]{:T(128)S(6)} %mul.112, pred[2048]{0:T(1024)(128)(4,1)S(1)} %get-tuple-element.73, pred[2048]{0:T(1024)(128)(4,1)S(1)} %get-tuple-element.74, pred[2048]{0:T(1024)(128)(4,1)S(1)} %get-tuple-element.75, pred[2048]{0:T(1024)(128)(4,1)S(1)} %get-tuple-element.76, ...), kind=kLoop, calls=%fused_computation.205 | loop fusion | flops 251904 | bytes 135400 | tf_op jit(solution)/shard_map/jit(_take)/and | solution.py:50
  138.5 0.2 compare_select_fusion
  138.7 54.1 %all-gather.2.cloned.1.call-done = bf16[8192,1024]{0,1:T(8,128)(2,1)} async-done(((bf16[256,1024]{0,1:T(8,128)(2,1)}), bf16[8192,1024]{0,1:T(8,128)(2,1)}) %all-gather.2.cloned.1.call-update) | async-done | bytes 16777232 | tf_op jit(solution)/shard_map/all_gather | solution.py:43
  192.8 22.4 %copy.9 = bf16[8192,1024]{1,0:T(8,128)(2,1)} copy(bf16[8192,1024]{0,1:T(8,128)(2,1)} %all-gather.2.cloned.1.call-done) | data formatting | bytes 33554432 | tf_op jit(solution)/shard_map/all_gather | solution.py:43
  215.2 14.0 %gather_fusion.1 = bf16[1024,1024]{1,0:T(8,128)(2,1)} fusion(bf16[8192,1024]{1,0:T(8,128)(2,1)} %copy.9, s32[1024]{0:T(1024)S(1)} %broadcast_clamp_fusion.1), kind=kCustom, calls=%fused_computation.1 | custom fusion | bytes 4198400 | tf_op jit(solution)/shard_map/jit(_take)/gather | solution.py:51
  229.2 18.9 %gather_fusion = bf16[2048,1024]{1,0:T(8,128)(2,1)} fusion(bf16[8192,1024]{1,0:T(8,128)(2,1)} %copy.9, s32[2048]{0:T(1024)S(1)} %broadcast_clamp_fusion), kind=kCustom, calls=%fused_computation | custom fusion | bytes 8396800 | tf_op jit(solution)/shard_map/jit(_take)/gather | solution.py:50
  248.0 0.6 mul.127
  248.6 1.6 copy-done.2
  250.2 0.7 copy-done.3
  250.9 10.0 %fusion = f32[2048,1024]{1,0:T(8,128)} fusion(f32[2048,1024]{1,0:T(8,128)} %param.5, f32[256,8,8,128]{3,2,1,0:T(8,128)S(1)} %bitcast.80, bf16[2048,1024]{1,0:T(8,128)(2,1)S(1)} %copy-done.2, pred[2048]{0:T(1024)(128)(4,1)S(1)} %get-tuple-element.7, bf16[1024,1024]{1,0:T(8,128)(2,1)S(1)} %copy-done.3, pred[1024]{0:T(1024)(128)(4,1)S(1)} %get-tuple-element.5), kind=kOutput, calls=%fused_computation.4 | convolution fusion | flops 4302307328 | bytes 31460352 | tf_op jit(solution)/shard_map/dot_general | solution.py:52
  (75 shorter events, 4.8 us)
Async XLA Ops:
  6.5 1.6 copy-start
  6.5 42.8 %copy-start.4 = (s32[16,8]{0,1:T(8,128)S(1)}, s32[16,8]{0,1:T(8,128)}, u32[]{:S(2)}) copy-start(s32[16,8]{0,1:T(8,128)} %param.9) | copy-start | bytes 1540
  6.5 42.9 %copy-start.5 = (s32[64]{0:T(128)S(1)}, s32[64]{0:T(128)}, u32[]{:S(2)}) copy-start(s32[64]{0:T(128)} %param.8) | copy-start | bytes 772
  6.5 42.8 %reduce-scatter.2.cloned.1.call-start = ((), (), s32[]{:S(2)}) async-start(), calls=%async_computation.1 | async-start | bytes 2621440 | tf_op jit(solution)/shard_map/reduce_scatter | solution.py:36
  11.3 181.5 %all-gather.2.cloned.1.call-start = ((), (), s32[]{:S(2)}) async-start(), calls=%async_computation.2 | async-start | bytes 17301504 | tf_op jit(solution)/shard_map/all_gather | solution.py:43
  248.0 2.2 copy-start.2
  248.0 2.9 %copy-start.3 = (bf16[1024,1024]{1,0:T(8,128)(2,1)S(1)}, bf16[1024,1024]{1,0:T(8,128)(2,1)}, u32[]{:S(2)}) copy-start(bf16[1024,1024]{1,0:T(8,128)(2,1)} %gather_fusion.1) | copy-start | bytes 6291460
  250.9 10.0 %copy-start.1 = (bf16[1024,1024]{1,0:T(8,128)(2,1)S(1)}, bf16[1024,1024]{1,0:T(8,128)(2,1)}, u32[]{:S(2)}) copy-start(bf16[1024,1024]{1,0:T(8,128)(2,1)} %param.7) | copy-start | bytes 6291460
Sparse Core Ops, SparseCore 0:
  11.4 37.9 reduce-scatter.1
  52.6 140.0 all-gather.1
where the time goes:
time: 270 us; the launch traced here: 268 us
  waiting for transfers between devices  92.2 us (34%)
  other arithmetic  85.5 us (32%)
  local copies, waits for them, and re-layouts  63.4 us (23%)
  between operations  13.5 us (5%)
  matrix products  13.1 us (5%)
    all_gather x1, waiting for transfers between devices, local(): all_blocks = lax.all_gather(own_block, ('row', 'col'), axis=0, tiled=True)  54.1 us
    reduce_scatter x1, waiting for transfers between devices, local(): lax.psum_scatter(times_inverse(panel_raw, inv_part).astype(jnp.bfloat16),...  38 us
    and x1, other arithmetic, local(): rows_panel = jnp.take(all_blocks, located(owner_of_rows), axis=0)  35.7 us
    and x1, other arithmetic, local(): cols_panel = jnp.take(all_blocks, located(owner_of_cols), axis=0)  35.6 us
    all_gather x1, local copies, waits for them, and re-layouts, local(): all_blocks = lax.all_gather(own_block, ('row', 'col'), axis=0, tiled=True)  22.4 us
    gather x1, local copies, waits for them, and re-layouts, local(): rows_panel = jnp.take(all_blocks, located(owner_of_rows), axis=0)  18.9 us
    gather x1, local copies, waits for them, and re-layouts, local(): cols_panel = jnp.take(all_blocks, located(owner_of_cols), axis=0)  14 us
    gather x60, other arithmetic, owner_row(): return position[global_ids // BLK] * BLK + global_ids % BLK  13.9 us
  transfers between devices with their start and end apart: 2, of which 2 were waited for; matrix products, arithmetic and copies ran while one was open for 33% of the time, Pallas kernels for 0%

commit v1 on v0

v1 whole, which is shorter than its diff:
```python
import functools

import jax
import jax.numpy as jnp
from jax import lax
from jax.experimental import pallas as pl
from jax.experimental.pallas import tpu as pltpu
from jax.sharding import PartitionSpec as P

BLK = 128
MESH = pl.DeviceIdType.MESH


def times_inverse(left, right):
    return lax.dot_general(
        left, right, (((1,), (1,)), ((), ())), preferred_element_type=jnp.float32
    )


def exchange_kernel(
    n_row, n_col, gpr,
    src_ref, raw_ref, d_hbm, rows_ref, cpan_ref,
    sorted_ref, a_ref, b_ref, own_ref, d_ref,
    a_send, a_recv, b_send, b_recv, c_send, c_recv, z_send, z_recv, f_send, f_recv, loc,
):
    r = lax.axis_index("row")
    c = lax.axis_index("col")
    n_pos = n_col // 2
    pos = c // 2
    core = c % 2
    sibling = pos * 2 + (1 - core)
    kw = raw_ref.shape[2]
    load_d = pltpu.make_async_copy(d_hbm, d_ref, loc.at[0])
    load_d.start()

    def remote(src, dst, ssem, rsem, rr, cc):
        return pltpu.make_async_remote_copy(
            src_ref=src, dst_ref=dst, send_sem=ssem, recv_sem=rsem,
            device_id=(rr, cc), device_id_type=MESH,
        )

    barrier = pltpu.get_barrier_semaphore()
    for dr in range(1, n_row):
        pl.semaphore_signal(barrier, inc=1, device_id=((r + dr) % n_row, c), device_id_type=MESH)
    for dc in range(1, n_col):
        pl.semaphore_signal(barrier, inc=1, device_id=(r, (c + dc) % n_col), device_id_type=MESH)
    for g in range(n_col):
        sorted_ref[g] = raw_ref[src_ref[g]]
    pl.semaphore_wait(barrier, n_row + n_col - 2)

    def a_copy(dr):
        to = (r + dr) % n_row
        return remote(sorted_ref.at[pl.ds(to * gpr, gpr)], a_ref.at[r],
                      a_send.at[dr], a_recv.at[dr], to, c)

    def b_copy(dc):
        to = (c + dc) % n_col
        return remote(sorted_ref.at[to], b_ref.at[c], b_send.at[dc], b_recv.at[dc], r, to)

    for dr in range(1, n_row):
        a_copy(dr).start()
    for dc in range(1, n_col):
        b_copy(dc).start()
    a_ref[r] = sorted_ref[pl.ds(r * gpr, gpr)]
    b_ref[c] = sorted_ref[c]
    load_d.wait()
    for dr in range(1, n_row):
        came = (r + n_row - dr) % n_row
        remote(sorted_ref.at[pl.ds(r * gpr, gpr)], a_ref.at[came],
               a_send.at[dr], a_recv.at[dr], (r + dr) % n_row, c).wait_recv()
    total = times_inverse(a_ref[0].reshape(gpr * BLK, kw), d_ref[:, :kw])
    for s in range(1, n_row):
        total += times_inverse(a_ref[s].reshape(gpr * BLK, kw), d_ref[:, s * kw:(s + 1) * kw])
    own_ref[...] = total.astype(jnp.bfloat16).reshape(own_ref.shape)

    def z_copy(dp):
        to = (pos + dp) % n_pos
        return remote(own_ref, rows_ref.at[c], z_send.at[dp], z_recv.at[dp], r, to * 2 + core)

    for dp in range(1, n_pos):
        z_copy(dp).start()
    f_own = remote(own_ref, rows_ref.at[c], f_send.at[0], f_recv.at[0], r, sibling)
    f_own.start()
    keep = pltpu.make_async_copy(own_ref, rows_ref.at[c], loc.at[1])
    keep.start()

    for dc in range(1, n_col):
        came = (c + n_col - dc) % n_col
        remote(sorted_ref.at[0], b_ref.at[came], b_send.at[dc], b_recv.at[dc],
               r, (c + dc) % n_col).wait_recv()

    def c_copy(dr):
        return remote(b_ref, cpan_ref.at[r], c_send.at[dr], c_recv.at[dr], (r + dr) % n_row, c)

    for dr in range(1, n_row):
        c_copy(dr).start()
    keep_c = pltpu.make_async_copy(b_ref, cpan_ref.at[r], loc.at[2])
    keep_c.start()

    def f_copy(dp):
        slot = ((pos + n_pos - dp) % n_pos) * 2 + core
        return remote(rows_ref.at[slot], rows_ref.at[slot], f_send.at[dp], f_recv.at[dp], r, sibling)

    for dp in range(1, n_pos):
        slot = ((pos + n_pos - dp) % n_pos) * 2 + core
        remote(own_ref, rows_ref.at[slot], z_send.at[dp], z_recv.at[dp],
               r, ((pos + dp) % n_pos) * 2 + core).wait_recv()
        f_copy(dp).start()
    for dp in range(n_pos):
        slot = ((pos + n_pos - dp) % n_pos) * 2 + (1 - core)
        remote(own_ref, rows_ref.at[slot], f_send.at[dp], f_recv.at[dp], r, sibling).wait_recv()
    for dr in range(1, n_row):
        came = (r + n_row - dr) % n_row
        remote(b_ref, cpan_ref.at[came], c_send.at[dr], c_recv.at[dr],
               (r + dr) % n_row, c).wait_recv()
    for dr in range(1, n_row):
        a_copy(dr).wait_send()
        c_copy(dr).wait_send()
    for dc in range(1, n_col):
        b_copy(dc).wait_send()
    f_own.wait_send()
    for dp in range(1, n_pos):
        z_copy(dp).wait_send()
        f_copy(dp).wait_send()
    keep.wait()
    keep_c.wait()


def update_kernel(
    n_row, block_cols,
    rows_idx, cols_idx, low_ref, high_ref, cpan_ref, d_ref, pat_ref, schur_ref, out_ref, cols_ref,
):
    kw = cpan_ref.shape[3]

    @pl.when(pl.program_id(0) == 0)
    def _():
        for w in range(block_cols):
            h = cols_idx[w]
            total = times_inverse(cpan_ref[0, h], d_ref[:, :kw])
            for s in range(1, n_row):
                total += times_inverse(cpan_ref[s, h], d_ref[:, s * kw:(s + 1) * kw])
            cols_ref[w * BLK:(w + 1) * BLK, :] = total.astype(jnp.bfloat16)

    left = jnp.concatenate([low_ref[0, 0], high_ref[0, 0]], axis=0)
    update = times_inverse(left, cols_ref[...])
    for e in range(2):
        part = slice(e * BLK, (e + 1) * BLK)
        out_ref[part, :] = schur_ref[part, :] - update[part, :] * pat_ref[e]


def local(schur, panel_raw, diag_inverse, perm, pattern):
    n_row = lax.axis_size("row")
    n_col = lax.axis_size("col")
    r = lax.axis_index("row")
    c = lax.axis_index("col")
    local_rows, local_cols = schur.shape
    block_rows, block_cols = local_rows // BLK, local_cols // BLK
    gpr = local_rows // local_cols
    held, kw = panel_raw.shape[0] // BLK, panel_raw.shape[1]
    snw = diag_inverse.shape[0]
    blocks = perm.shape[0]
    bf16 = jnp.bfloat16

    mine = lax.dynamic_slice_in_dim(perm, c * held, held, 0)
    group_of = mine // block_cols
    at = jnp.arange(held, dtype=jnp.int32)
    groups = jnp.arange(n_col, dtype=jnp.int32)
    source = jnp.sum(jnp.where(group_of[None, :] == groups[:, None], at[None, :], 0), axis=1)
    holder = jnp.arange(blocks, dtype=jnp.int32) // held

    def holders_of(first, count):
        ids = first + jnp.arange(count, dtype=jnp.int32)
        return jnp.sum(jnp.where(perm[None, :] == ids[:, None], holder[None, :], 0), axis=1)

    rows_idx = holders_of(r * block_rows, block_rows)
    cols_idx = holders_of(c * block_cols, block_cols)
    n_pos = n_col // 2
    dma = pltpu.SemaphoreType.DMA
    rows, cpan = pl.pallas_call(
        functools.partial(exchange_kernel, n_row, n_col, gpr),
        out_shape=(
            jax.ShapeDtypeStruct((n_col, gpr, BLK, snw), bf16),
            jax.ShapeDtypeStruct((n_row, n_col, BLK, kw), bf16),
        ),
        in_specs=[
            pl.BlockSpec(memory_space=pltpu.SMEM),
            pl.BlockSpec(memory_space=pltpu.VMEM),
            pl.BlockSpec(memory_space=pl.ANY),
        ],
        out_specs=(pl.BlockSpec(memory_space=pl.ANY), pl.BlockSpec(memory_space=pl.ANY)),
        scratch_shapes=[
            pltpu.VMEM((n_col, BLK, kw), bf16),
            pltpu.VMEM((n_row, gpr, BLK, kw), bf16),
            pltpu.VMEM((n_col, BLK, kw), bf16),
            pltpu.VMEM((gpr, BLK, snw), bf16),
            pltpu.VMEM((snw, snw), bf16),
            dma((n_row,)), dma((n_row,)), dma((n_col,)), dma((n_col,)),
            dma((n_row,)), dma((n_row,)), dma((n_pos,)), dma((n_pos,)),
            dma((n_pos,)), dma((n_pos,)), dma((3,)),
        ],
        compiler_params=pltpu.CompilerParams(
            collective_id=0, has_side_effects=True, vmem_limit_bytes=32 * 2**20
        ),
    )(source, panel_raw.reshape(held, BLK, kw), diag_inverse)

    weights = jnp.repeat(pattern.astype(jnp.float32), BLK, axis=1)[:, None, :]

    def row_spec(e):
        return pl.BlockSpec(
            (1, 1, BLK, snw),
            lambda i, ri, ci: (ri[2 * i + e], (2 * i + e) // block_cols, 0, 0),
        )

    return pl.pallas_call(
        functools.partial(update_kernel, n_row, block_cols),
        out_shape=jax.ShapeDtypeStruct(schur.shape, schur.dtype),
        grid_spec=pltpu.PrefetchScalarGridSpec(
            num_scalar_prefetch=2,
            grid=(block_rows // 2,),
            in_specs=[
                row_spec(0),
                row_spec(1),
                pl.BlockSpec((n_row, n_col, BLK, kw), lambda i, ri, ci: (0, 0, 0, 0)),
                pl.BlockSpec((snw, snw), lambda i, ri, ci: (0, 0)),
                pl.BlockSpec((2, 1, local_cols), lambda i, ri, ci: (i, 0, 0)),
                pl.BlockSpec((2 * BLK, local_cols), lambda i, ri, ci: (i, 0)),
            ],
            out_specs=pl.BlockSpec((2 * BLK, local_cols), lambda i, ri, ci: (i, 0)),
            scratch_shapes=[pltpu.VMEM((local_cols, snw), bf16)],
        ),
        compiler_params=pltpu.CompilerParams(vmem_limit_bytes=40 * 2**20),
    )(rows_idx, cols_idx, rows, rows, cpan, diag_inverse, weights, schur)


def solution(mesh):
    return jax.shard_map(
        local,
        mesh=mesh,
        in_specs=(P("row", "col"), P("col", "row"), P(), P(), P("row", "col")),
        out_specs=P("row", "col"),
        check_vma=False,
    )
```

time: 270 us -> 89.6 us (0.33)
  the two profiles are of different devices: /device:TPU:0 before, /device:TPU:31 now
where the time goes in v1:
time: 89.6 us; the launch traced here: 89.1 us
  Pallas kernels  81.4 us (91%)
  local copies, waits for them, and re-layouts  4.37 us (5%)
  other arithmetic  3.23 us (4%)
    pallas_call x1, Pallas kernels, local(): pl.pallas_call(functools.partial(exchange_kernel, n_row, n_col, gpr), out...  64.2 us
    pallas_call x1, Pallas kernels, local(): pl.pallas_call(functools.partial(update_kernel, n_row, block_cols), out_s...  17.2 us
    unnamed x6, local copies, waits for them, and re-layouts  4.22 us

profile of v1, /device:TPU:31, one launch (start us, length us, event | category | flops | bytes accessed | tf_op | source)
XLA Modules:
  0.0 89.1 jit_solution(16809663172585495409)
XLA Ops:
  0.0 0.7 and_select_fusion
  0.7 0.1 select_reduce_fusion.1.src_ref
  0.9 0.8 select_reduce_fusion.2.cols_idx
  1.7 0.8 select_reduce_fusion.rows_idx
  2.6 0.7 convert_element_type.3
  3.3 0.1 copy.7
  3.3 0.1 broadcast_in_dim.54
  3.4 0.0 copy-start
  3.4 1.6 %copy-done = bf16[1024,1024]{1,0:T(8,128)(2,1)S(1)} copy-done((bf16[1024,1024]{1,0:T(8,128)(2,1)S(1)}, bf16[1024,1024]{1,0:T(8,128)(2,1)}, u32[]{:S(2)}) %copy-start) | copy-done | bytes 2097176
  5.0 0.0 copy-start.2
  5.0 1.0 %copy-done.2 = bf16[1024,256]{1,0:T(8,128)(2,1)S(1)} copy-done((bf16[1024,256]{1,0:T(8,128)(2,1)S(1)}, bf16[1024,256]{1,0:T(8,128)(2,1)}, u32[]{:S(2)}) %copy-start.2) | copy-done | bytes 524312
  6.0 64.2 %shard_map.55 = (bf16[8,2,128,1024]{3,2,1,0:T(8,128)(2,1)S(1)}, bf16[4,8,128,256]{3,2,1,0:T(8,128)(2,1)S(1)}) custom-call(s32[8]{0:T(128)S(1)} %select_reduce_fusion.1.src_ref, bf16[8,128,256]{2,1,0:T(8,128)(2,1)S(1)} %bitcast.2, bf16[1024,1024]{1,0:T(8,128)(2,1)S(1)} %copy-done), custom_call_target="tpu_custom_call" | custom-call | tf_op jit(solution)/shard_map/pallas_call | solution.py:179
  70.3 0.0 copy-start.1
  70.3 1.6 %copy-done.1 = bf16[1024,1024]{1,0:T(8,128)(2,1)S(1)} copy-done((bf16[1024,1024]{1,0:T(8,128)(2,1)S(1)}, bf16[1024,1024]{1,0:T(8,128)(2,1)}, u32[]{:S(2)}) %copy-start.1) | copy-done | bytes 2097176
  71.9 17.2 %shard_map.56 = f32[2048,1024]{1,0:T(8,128)} custom-call(s32[16]{0:T(128)S(1)} %select_reduce_fusion.rows_idx, s32[8]{0:T(128)S(1)} %select_reduce_fusion.2.cols_idx, bf16[8,2,128,1024]{3,2,1,0:T(8,128)(2,1)S(1)} %get-tuple-element.7.low_ref.high_ref, bf16[8,2,128,1024]{3,2,1,0:T(8,128)(2,1)S(1)} %get-tuple-element.7.low_ref.high_ref, ...), custom_call_target="tpu_custom_call" | custom-call | tf_op jit(solution)/shard_map/pallas_call | solution.py:214
  (3 shorter events, 0.0 us)
Async XLA Ops:
  3.4 1.6 %copy-start = (bf16[1024,1024]{1,0:T(8,128)(2,1)S(1)}, bf16[1024,1024]{1,0:T(8,128)(2,1)}, u32[]{:S(2)}) copy-start(bf16[1024,1024]{1,0:T(8,128)(2,1)} %d_ref.1) | copy-start | bytes 6291460
  5.0 1.0 %copy-start.2 = (bf16[1024,256]{1,0:T(8,128)(2,1)S(1)}, bf16[1024,256]{1,0:T(8,128)(2,1)}, u32[]{:S(2)}) copy-start(bf16[1024,256]{1,0:T(8,128)(2,1)} %param.6) | copy-start | bytes 1572868
  70.3 1.6 %copy-start.1 = (bf16[1024,1024]{1,0:T(8,128)(2,1)S(1)}, bf16[1024,1024]{1,0:T(8,128)(2,1)}, u32[]{:S(2)}) copy-start(bf16[1024,1024]{1,0:T(8,128)(2,1)} %d_ref.1) | copy-start | bytes 6291460

commit v2 on v1

v2 whole, which is shorter than its diff:
```python
import functools

import jax
import jax.numpy as jnp
from jax import lax
from jax.experimental import pallas as pl
from jax.experimental.pallas import tpu as pltpu
from jax.sharding import PartitionSpec as P

BLK = 128
MESH = pl.DeviceIdType.MESH


def times_inverse(left, right):
    return lax.dot_general(
        left, right, (((1,), (1,)), ((), ())), preferred_element_type=jnp.float32
    )


def exchange_kernel(
    n_row, n_col, gpr, held, block_cols,
    perm_ref, table_ref, raw_hbm, d_hbm, rows_ref, cols_ref,
    raw_ref, sorted_ref, a_ref, b_ref, own_ref, d_ref, cpan_ref,
    a_send, a_recv, b_send, b_recv, c_send, c_recv,
    up_send, up_recv, down_send, down_recv, f_send, f_recv, loc,
):
    r = lax.axis_index("row")
    c = lax.axis_index("col")
    n_pos = n_col // 2
    pos = c // 2
    core = c % 2
    sibling = pos * 2 + (1 - core)
    kw = raw_ref.shape[2]
    snw = d_ref.shape[0]
    load_raw = pltpu.make_async_copy(raw_hbm, raw_ref, loc.at[3])
    load_raw.start()
    load_d = pltpu.make_async_copy(d_hbm, d_ref, loc.at[0])
    load_d.start()

    def remote(src, dst, ssem, rsem, rr, cc):
        return pltpu.make_async_remote_copy(
            src_ref=src, dst_ref=dst, send_sem=ssem, recv_sem=rsem,
            device_id=(rr, cc), device_id_type=MESH,
        )

    def part(index):
        return pl.ds(pl.multiple_of(index * kw, kw), kw)

    barrier = pltpu.get_barrier_semaphore()
    for dr in range(1, n_row):
        pl.semaphore_signal(barrier, inc=1, device_id=((r + dr) % n_row, c), device_id_type=MESH)
    for dc in range(1, n_col):
        pl.semaphore_signal(barrier, inc=1, device_id=(r, (c + dc) % n_col), device_id_type=MESH)
    groups = [lax.div(perm_ref[c * held + i], block_cols) for i in range(held)]
    load_raw.wait()
    for g in range(n_col):
        block = 0
        for i in range(1, held):
            block = jnp.where(groups[i] == g, i, block)
        sorted_ref[g] = raw_ref[block]
    pl.semaphore_wait(barrier, n_row + n_col - 2)

    def a_copy(dr, came=None):
        to = (r + dr) % n_row
        return remote(sorted_ref.at[pl.ds(to * gpr, gpr)],
                      a_ref.at[:, :, part(r if came is None else came)],
                      a_send.at[dr], a_recv.at[dr], to, c)

    def b_copy(dc, came=None):
        to = (c + dc) % n_col
        return remote(sorted_ref.at[to], b_ref.at[c if came is None else came],
                      b_send.at[dc], b_recv.at[dc], r, to)

    for dr in range(1, n_row):
        a_copy(dr).start()
    for dc in range(1, n_col):
        b_copy(dc).start()
    a_ref[:, :, part(r)] = sorted_ref[pl.ds(r * gpr, gpr)]
    b_ref[c] = sorted_ref[c]
    load_d.wait()
    for dr in range(1, n_row):
        a_copy(dr, (r + n_row - dr) % n_row).wait_recv()
    own = times_inverse(a_ref[...].reshape(gpr * BLK, snw), d_ref[...])
    own_ref[...] = own.astype(jnp.bfloat16).reshape(own_ref.shape)

    def up_copy(d):
        slot = (pos - d) * 2 + core
        return remote(own_ref if d == 0 else rows_ref.at[slot], rows_ref.at[slot],
                      up_send.at[d], up_recv.at[d], r, (pos + 1) * 2 + core)

    def down_copy(d):
        slot = (pos + d) * 2 + core
        return remote(own_ref if d == 0 else rows_ref.at[slot], rows_ref.at[slot],
                      down_send.at[d], down_recv.at[d], r, (pos - 1) * 2 + core)

    def side_copy(source, mine):
        slot = source * 2 + core
        return remote(own_ref if mine else rows_ref.at[slot], rows_ref.at[slot],
                      f_send.at[source], f_recv.at[source], r, sibling)

    @pl.when(pos < n_pos - 1)
    def _():
        up_copy(0).start()

    @pl.when(pos > 0)
    def _():
        down_copy(0).start()

    side_copy(pos, True).start()
    keep = pltpu.make_async_copy(own_ref, rows_ref.at[c], loc.at[1])
    keep.start()

    for dc in range(1, n_col):
        b_copy(dc, (c + n_col - dc) % n_col).wait_recv()

    def c_copy(dr, came=None):
        return remote(b_ref, cpan_ref.at[:, :, part(r if came is None else came)],
                      c_send.at[dr], c_recv.at[dr], (r + dr) % n_row, c)

    for dr in range(1, n_row):
        c_copy(dr).start()
    cpan_ref[:, :, part(r)] = b_ref[...]

    def factor_columns():
        for dr in range(1, n_row):
            c_copy(dr, (r + n_row - dr) % n_row).wait_recv()
        step = 4 if block_cols % 4 == 0 else 1
        for w in range(0, block_cols, step):
            left = jnp.concatenate([cpan_ref[table_ref[w + k]] for k in range(step)], axis=0)
            done = times_inverse(left, d_ref[...]).astype(jnp.bfloat16)
            cols_ref[w * BLK:(w + step) * BLK, :] = done

    for d in range(1, n_pos):
        if d == n_pos - 1:
            factor_columns()

        @pl.when(pos - d >= 0)
        def _(d=d):
            slot = (pos - d) * 2 + core
            remote(own_ref, rows_ref.at[slot], up_send.at[d - 1], up_recv.at[d - 1],
                   r, sibling).wait_recv()
            if d < n_pos - 1:
                @pl.when(pos < n_pos - 1)
                def _():
                    up_copy(d).start()
            side_copy(pos - d, False).start()

        @pl.when(pos + d <= n_pos - 1)
        def _(d=d):
            slot = (pos + d) * 2 + core
            remote(own_ref, rows_ref.at[slot], down_send.at[d - 1], down_recv.at[d - 1],
                   r, sibling).wait_recv()
            if d < n_pos - 1:
                @pl.when(pos > 0)
                def _():
                    down_copy(d).start()
            side_copy(pos + d, False).start()

    for dr in range(1, n_row):
        a_copy(dr).wait_send()
        c_copy(dr).wait_send()
    for dc in range(1, n_col):
        b_copy(dc).wait_send()
    for d in range(n_pos - 1):
        @pl.when((pos - d >= 0) & (pos < n_pos - 1))
        def _(d=d):
            up_copy(d).wait_send()

        @pl.when((pos + d <= n_pos - 1) & (pos > 0))
        def _(d=d):
            down_copy(d).wait_send()
    for source in range(n_pos):
        slot = source * 2 + (1 - core)
        remote(own_ref, rows_ref.at[slot], f_send.at[source], f_recv.at[source],
               r, sibling).wait_recv()
        side_copy(source, True).wait_send()
    keep.wait()


def update_kernel(
    table, pat_ref, low_ref, high_ref, cols_ref, schur_ref, out_ref,
):
    i = pl.program_id(0)
    left = jnp.concatenate([low_ref[0, 0], high_ref[0, 0]], axis=0)
    update = times_inverse(left, cols_ref[...])
    for e in range(2):
        rows = slice(e * BLK, (e + 1) * BLK)
        for w in range(cols_ref.shape[0] // BLK):
            at = slice(w * BLK, (w + 1) * BLK)
            weight = pat_ref[2 * i + e, w].astype(jnp.float32)
            out_ref[rows, at] = schur_ref[rows, at] - update[rows, at] * weight


def local(schur, panel_raw, diag_inverse, perm, pattern):
    n_row = lax.axis_size("row")
    n_col = lax.axis_size("col")
    r = lax.axis_index("row")
    c = lax.axis_index("col")
    local_rows, local_cols = schur.shape
    block_rows, block_cols = local_rows // BLK, local_cols // BLK
    gpr = local_rows // local_cols
    held, kw = panel_raw.shape[0] // BLK, panel_raw.shape[1]
    snw = diag_inverse.shape[0]
    blocks = perm.shape[0]
    bf16 = jnp.bfloat16

    at = jnp.arange(block_cols + block_rows, dtype=jnp.int32)
    ids = jnp.where(at < block_cols, c * block_cols + at, r * block_rows + at - block_cols)
    holder = lax.div(lax.broadcasted_iota(jnp.int32, (ids.shape[0], blocks), 1), held)
    table = jnp.sum(jnp.where(perm[None, :] == ids[:, None], holder, 0), axis=1)
    n_pos = n_col // 2
    dma = pltpu.SemaphoreType.DMA
    smem = pl.BlockSpec(memory_space=pltpu.SMEM)
    hbm = pl.BlockSpec(memory_space=pltpu.HBM)
    rows, cols = pl.pallas_call(
        functools.partial(exchange_kernel, n_row, n_col, gpr, held, block_cols),
        out_shape=(
            jax.ShapeDtypeStruct((n_col, gpr, BLK, snw), bf16),
            jax.ShapeDtypeStruct((local_cols, snw), bf16),
        ),
        in_specs=[smem, smem, hbm, hbm],
        out_specs=(
            pl.BlockSpec(memory_space=pl.ANY),
            pl.BlockSpec(memory_space=pltpu.VMEM),
        ),
        scratch_shapes=[
            pltpu.VMEM((held, BLK, kw), bf16),
            pltpu.VMEM((n_col, BLK, kw), bf16),
            pltpu.VMEM((gpr, BLK, snw), bf16),
            pltpu.VMEM((n_col, BLK, kw), bf16),
            pltpu.VMEM((gpr, BLK, snw), bf16),
            pltpu.VMEM((snw, snw), bf16),
            pltpu.VMEM((n_col, BLK, snw), bf16),
            dma((n_row,)), dma((n_row,)), dma((n_col,)), dma((n_col,)),
            dma((n_row,)), dma((n_row,)), dma((n_pos,)), dma((n_pos,)),
            dma((n_pos,)), dma((n_pos,)), dma((n_pos,)), dma((n_pos,)), dma((4,)),
        ],
        compiler_params=pltpu.CompilerParams(
            collective_id=0, has_side_effects=True, vmem_limit_bytes=32 * 2**20
        ),
    )(perm, table, panel_raw.reshape(held, BLK, kw), diag_inverse)

    def row_spec(e):
        return pl.BlockSpec(
            (1, 1, BLK, snw),
            lambda i, t, p: (t[block_cols + 2 * i + e], (2 * i + e) // block_cols, 0, 0),
        )

    return pl.pallas_call(
        update_kernel,
        out_shape=jax.ShapeDtypeStruct(schur.shape, schur.dtype),
        grid_spec=pltpu.PrefetchScalarGridSpec(
            num_scalar_prefetch=2,
            grid=(block_rows // 2,),
            in_specs=[
                row_spec(0),
                row_spec(1),
                pl.BlockSpec((local_cols, snw), lambda i, t, p: (0, 0)),
                pl.BlockSpec((2 * BLK, local_cols), lambda i, t, p: (i, 0)),
            ],
            out_specs=pl.BlockSpec((2 * BLK, local_cols), lambda i, t, p: (i, 0)),
        ),
        compiler_params=pltpu.CompilerParams(vmem_limit_bytes=32 * 2**20),
    )(table, pattern, rows, rows, cols, schur)


def solution(mesh):
    return jax.shard_map(
        local,
        mesh=mesh,
        in_specs=(P("row", "col"), P("col", "row"), P(), P(), P("row", "col")),
        out_specs=P("row", "col"),
        check_vma=False,
    )
```

time: 89.6 us -> 73.3 us (0.82)
  the two profiles are of different devices: /device:TPU:31 before, /device:TPU:0 now
where the time goes in v2:
time: 73.3 us; the launch traced here: 73 us
  Pallas kernels  64.7 us (88%)
  local copies, waits for them, and re-layouts  7.43 us (10%)
  other arithmetic  0.84 us (1%)
    pallas_call x1, Pallas kernels, local(): pl.pallas_call(functools.partial(exchange_kernel, n_row, n_col, gpr, held...  56.4 us
    pallas_call x1, Pallas kernels, local(): pl.pallas_call(update_kernel, out_shape=jax.ShapeDtypeStruct(schur.shape,...  8.36 us
    unnamed x9, local copies, waits for them, and re-layouts  7.43 us

profile of v2, /device:TPU:0, one launch (start us, length us, event | category | flops | bytes accessed | tf_op | source)
XLA Modules:
  0.0 73.0 jit_solution(10090407812706159326)
XLA Ops:
  0.0 0.8 %select_reduce_fusion.table_ref.table = s32[24]{0:T(128)S(1)} fusion(s32[64]{0:T(128)S(1)} %iota_shift-right-logical_fusion, s32[64]{0:T(128)} %perm_ref.1, s32[24]{0:T(128)S(1)} %compare_select_fusion), kind=kLoop, calls=%fused_computation | loop fusion | flops 4584 | bytes 704 | tf_op jit(solution)/shard_map/reduce_sum | solution.py:210
  0.8 0.8 %copy.7.pat_ref = s32[16,8]{1,0:T(8,128)S(1)} copy(s32[16,8]{0,1:T(8,128)} %param.9) | data formatting | bytes 1024 | tf_op args[4]
  1.6 0.0 copy-start.1
  1.6 1.6 %copy-done.1 = bf16[1024,1024]{1,0:T(8,128)(2,1)S(1)} copy-done((bf16[1024,1024]{1,0:T(8,128)(2,1)S(1)}, bf16[1024,1024]{1,0:T(8,128)(2,1)}, u32[]{:S(2)}) %copy-start.1) | copy-done | bytes 2097176
  3.2 0.0 copy-start.2
  3.2 1.0 %copy-done.2 = bf16[1024,256]{1,0:T(8,128)(2,1)S(1)} copy-done((bf16[1024,256]{1,0:T(8,128)(2,1)S(1)}, bf16[1024,256]{1,0:T(8,128)(2,1)}, u32[]{:S(2)}) %copy-start.2) | copy-done | bytes 524312
  4.2 0.0 copy-start.3
  4.2 0.7 copy-done.3
  4.9 56.4 %shard_map.55 = (bf16[8,2,128,1024]{3,2,1,0:T(8,128)(2,1)S(1)}, bf16[1024,1024]{1,0:T(8,128)(2,1)S(1)}) custom-call(s32[64]{0:T(128)S(1)} %copy-done.3, s32[24]{0:T(128)S(1)} %select_reduce_fusion.table_ref.table, bf16[8,128,256]{2,1,0:T(8,128)(2,1)S(1)} %bitcast.1, bf16[1024,1024]{1,0:T(8,128)(2,1)S(1)} %copy-done.1), custom_call_target="tpu_custom_call" | custom-call | tf_op jit(solution)/shard_map/pallas_call | solution.py:215
  61.3 0.0 copy-start
  61.3 3.4 %copy-done = f32[2048,1024]{1,0:T(8,128)S(1)} copy-done((f32[2048,1024]{1,0:T(8,128)S(1)}, f32[2048,1024]{1,0:T(8,128)}, u32[]{:S(2)}) %copy-start) | copy-done | bytes 8388632
  64.7 8.4 %shard_map.56 = f32[2048,1024]{1,0:T(8,128)} custom-call(s32[24]{0:T(128)S(1)} %select_reduce_fusion.table_ref.table, s32[16,8]{1,0:T(8,128)S(1)} %copy.7.pat_ref, bf16[8,2,128,1024]{3,2,1,0:T(8,128)(2,1)S(1)} %get-tuple-element.7.low_ref.high_ref, bf16[8,2,128,1024]{3,2,1,0:T(8,128)(2,1)S(1)} %get-tuple-element.7.low_ref.high_ref, ...), custom_call_target="tpu_custom_call" | custom-call | tf_op jit(solution)/shard_map/pallas_call | solution.py:249
  (2 shorter events, 0.0 us)
Async XLA Ops:
  1.6 1.6 %copy-start.1 = (bf16[1024,1024]{1,0:T(8,128)(2,1)S(1)}, bf16[1024,1024]{1,0:T(8,128)(2,1)}, u32[]{:S(2)}) copy-start(bf16[1024,1024]{1,0:T(8,128)(2,1)} %d_hbm.1) | copy-start | bytes 6291460
  3.2 1.0 %copy-start.2 = (bf16[1024,256]{1,0:T(8,128)(2,1)S(1)}, bf16[1024,256]{1,0:T(8,128)(2,1)}, u32[]{:S(2)}) copy-start(bf16[1024,256]{1,0:T(8,128)(2,1)} %param.6) | copy-start | bytes 1572868
  4.2 0.7 copy-start.3
  61.3 3.4 %copy-start = (f32[2048,1024]{1,0:T(8,128)S(1)}, f32[2048,1024]{1,0:T(8,128)}, u32[]{:S(2)}) copy-start(f32[2048,1024]{1,0:T(8,128)} %schur_ref.1) | copy-start | bytes 25165828

commit v3 on v2

--- a/solution.py
+++ b/solution.py
@@ -80,33 +80,34 @@
     load_d.wait()
     for dr in range(1, n_row):
         a_copy(dr, (r + n_row - dr) % n_row).wait_recv()
-    own = times_inverse(a_ref[...].reshape(gpr * BLK, snw), d_ref[...])
-    own_ref[...] = own.astype(jnp.bfloat16).reshape(own_ref.shape)
-
-    def up_copy(d):
+    def up_copy(d, q):
         slot = (pos - d) * 2 + core
-        return remote(own_ref if d == 0 else rows_ref.at[slot], rows_ref.at[slot],
-                      up_send.at[d], up_recv.at[d], r, (pos + 1) * 2 + core)
-
-    def down_copy(d):
+        return remote(own_ref.at[q] if d == 0 else rows_ref.at[slot, q], rows_ref.at[slot, q],
+                      up_send.at[d, q], up_recv.at[d, q], r, (pos + 1) * 2 + core)
+
+    def down_copy(d, q):
         slot = (pos + d) * 2 + core
-        return remote(own_ref if d == 0 else rows_ref.at[slot], rows_ref.at[slot],
-                      down_send.at[d], down_recv.at[d], r, (pos - 1) * 2 + core)
-
-    def side_copy(source, mine):
+        return remote(own_ref.at[q] if d == 0 else rows_ref.at[slot, q], rows_ref.at[slot, q],
+                      down_send.at[d, q], down_recv.at[d, q], r, (pos - 1) * 2 + core)
+
+    def side_copy(source, q, mine):
         slot = source * 2 + core
-        return remote(own_ref if mine else rows_ref.at[slot], rows_ref.at[slot],
-                      f_send.at[source], f_recv.at[source], r, sibling)
-
-    @pl.when(pos < n_pos - 1)
-    def _():
-        up_copy(0).start()
-
-    @pl.when(pos > 0)
-    def _():
-        down_copy(0).start()
-
-    side_copy(pos, True).start()
+        return remote(own_ref.at[q] if mine else rows_ref.at[slot, q], rows_ref.at[slot, q],
+                      f_send.at[source, q], f_recv.at[source, q], r, sibling)
+
+    for q in range(gpr):
+        own_ref[q] = times_inverse(a_ref[q], d_ref[...]).astype(jnp.bfloat16)
+
+        @pl.when(pos < n_pos - 1)
+        def _(q=q):
+            up_copy(0, q).start()
+
+        @pl.when(pos > 0)
+        def _(q=q):
+            down_copy(0, q).start()
+
+    for q in range(gpr):
+        side_copy(pos, q, True).start()
     keep = pltpu.make_async_copy(own_ref, rows_ref.at[c], loc.at[1])
     keep.start()
 
@@ -134,46 +135,48 @@
         if d == n_pos - 1:
             factor_columns()
 
-        @pl.when(pos - d >= 0)
-        def _(d=d):
-            slot = (pos - d) * 2 + core
-            remote(own_ref, rows_ref.at[slot], up_send.at[d - 1], up_recv.at[d - 1],
-                   r, sibling).wait_recv()
-            if d < n_pos - 1:
-                @pl.when(pos < n_pos - 1)
-                def _():
-                    up_copy(d).start()
-            side_copy(pos - d, False).start()
-
-        @pl.when(pos + d <= n_pos - 1)
-        def _(d=d):
-            slot = (pos + d) * 2 + core
-            remote(own_ref, rows_ref.at[slot], down_send.at[d - 1], down_recv.at[d - 1],
-                   r, sibling).wait_recv()
-            if d < n_pos - 1:
-                @pl.when(pos > 0)
-                def _():
-                    down_copy(d).start()
-            side_copy(pos + d, False).start()
+        for q in range(gpr):
+            @pl.when(pos - d >= 0)
+            def _(d=d, q=q):
+                slot = (pos - d) * 2 + core
+                remote(own_ref.at[q], rows_ref.at[slot, q], up_send.at[d - 1, q],
+                       up_recv.at[d - 1, q], r, sibling).wait_recv()
+                if d < n_pos - 1:
+                    @pl.when(pos < n_pos - 1)
+                    def _():
+                        up_copy(d, q).start()
+                side_copy(pos - d, q, False).start()
+
+            @pl.when(pos + d <= n_pos - 1)
+            def _(d=d, q=q):
+                slot = (pos + d) * 2 + core
+                remote(own_ref.at[q], rows_ref.at[slot, q], down_send.at[d - 1, q],
+                       down_recv.at[d - 1, q], r, sibling).wait_recv()
+                if d < n_pos - 1:
+                    @pl.when(pos > 0)
+                    def _():
+                        down_copy(d, q).start()
+                side_copy(pos + d, q, False).start()
 
     for dr in range(1, n_row):
         a_copy(dr).wait_send()
         c_copy(dr).wait_send()
     for dc in range(1, n_col):
         b_copy(dc).wait_send()
-    for d in range(n_pos - 1):
-        @pl.when((pos - d >= 0) & (pos < n_pos - 1))
-        def _(d=d):
-            up_copy(d).wait_send()
-
-        @pl.when((pos + d <= n_pos - 1) & (pos > 0))
-        def _(d=d):
-            down_copy(d).wait_send()
-    for source in range(n_pos):
-        slot = source * 2 + (1 - core)
-        remote(own_ref, rows_ref.at[slot], f_send.at[source], f_recv.at[source],
-               r, sibling).wait_recv()
-        side_copy(source, True).wait_send()
+    for q in range(gpr):
+        for d in range(n_pos - 1):
+            @pl.when((pos - d >= 0) & (pos < n_pos - 1))
+            def _(d=d, q=q):
+                up_copy(d, q).wait_send()
+
+            @pl.when((pos + d <= n_pos - 1) & (pos > 0))
+            def _(d=d, q=q):
+                down_copy(d, q).wait_send()
+        for source in range(n_pos):
+            slot = source * 2 + (1 - core)
+            remote(own_ref.at[q], rows_ref.at[slot, q], f_send.at[source, q],
+                   f_recv.at[source, q], r, sibling).wait_recv()
+            side_copy(source, q, True).wait_send()
     keep.wait()
 
 
@@ -232,11 +235,16 @@
             pltpu.VMEM((snw, snw), bf16),
             pltpu.VMEM((n_col, BLK, snw), bf16),
             dma((n_row,)), dma((n_row,)), dma((n_col,)), dma((n_col,)),
-            dma((n_row,)), dma((n_row,)), dma((n_pos,)), dma((n_pos,)),
-            dma((n_pos,)), dma((n_pos,)), dma((n_pos,)), dma((n_pos,)), dma((4,)),
+            dma((n_row,)), dma((n_row,)), dma((n_pos, gpr)), dma((n_pos, gpr)),
+            dma((n_pos, gpr)), dma((n_pos, gpr)), dma((n_pos, gpr)), dma((n_pos, gpr)), dma((4,)),
         ],
         compiler_params=pltpu.CompilerParams(
-            collective_id=0, has_side_effects=True, vmem_limit_bytes=32 * 2**20
+            collective_id=0, has_side_effects=True, vmem_limit_bytes=20 * 2**20
+        ),
+        cost_estimate=pl.CostEstimate(
+            flops=2 * (local_cols + gpr * BLK) * snw * snw,
+            bytes_accessed=30 * local_rows * snw,
+            transcendentals=0,
         ),
     )(perm, table, panel_raw.reshape(held, BLK, kw), diag_inverse)
 
@@ -260,7 +268,7 @@
             ],
             out_specs=pl.BlockSpec((2 * BLK, local_cols), lambda i, t, p: (i, 0)),
         ),
-        compiler_params=pltpu.CompilerParams(vmem_limit_bytes=32 * 2**20),
+        compiler_params=pltpu.CompilerParams(vmem_limit_bytes=20 * 2**20),
     )(table, pattern, rows, rows, cols, schur)
 
 

time: 73.3 us -> 65.7 us (0.90)
  Pallas kernels: 64.7 us -> 60.5 us
  local copies, waits for them, and re-layouts: 7.43 us -> 4.05 us
    pallas_call x1, Pallas kernels: 56.4 us -> 52.2 us  [local(): pl.pallas_call(functools.partial(exchange_kernel, n_row, n_col, gpr, held...]
    unnamed x9, local copies, waits for them, and re-layouts: 7.43 us -> 4.05 us
where the time goes in v3:
time: 65.7 us; the launch traced here: 65.4 us
  Pallas kernels  60.5 us (92%)
  local copies, waits for them, and re-layouts  4.05 us (6%)
  other arithmetic  0.84 us (1%)
    pallas_call x1, Pallas kernels, local(): pl.pallas_call(functools.partial(exchange_kernel, n_row, n_col, gpr, held...  52.2 us
    pallas_call x1, Pallas kernels, local(): pl.pallas_call(update_kernel, out_shape=jax.ShapeDtypeStruct(schur.shape,...  8.37 us
    unnamed x9, local copies, waits for them, and re-layouts  4.05 us

profile of v3, /device:TPU:0, one launch (start us, length us, event | category | flops | bytes accessed | tf_op | source)
XLA Modules:
  0.0 65.4 jit_solution(12187718672505688584)
XLA Ops:
  0.0 0.8 %select_reduce_fusion.table_ref.table = s32[24]{0:T(128)S(1)} fusion(s32[64]{0:T(128)S(1)} %iota_shift-right-logical_fusion, s32[64]{0:T(128)} %perm_ref.1, s32[24]{0:T(128)S(1)} %compare_select_fusion), kind=kLoop, calls=%fused_computation | loop fusion | flops 4584 | bytes 704 | tf_op jit(solution)/shard_map/reduce_sum | solution.py:213
  0.8 0.8 %copy.7.pat_ref = s32[16,8]{1,0:T(8,128)S(1)} copy(s32[16,8]{0,1:T(8,128)} %param.9) | data formatting | bytes 1024 | tf_op args[4]
  1.6 0.0 copy-start.1
  1.6 0.7 copy-done.1
  2.3 0.0 copy-start.2
  2.3 1.6 %copy-done.2 = bf16[1024,1024]{1,0:T(8,128)(2,1)S(1)} copy-done((bf16[1024,1024]{1,0:T(8,128)(2,1)S(1)}, bf16[1024,1024]{1,0:T(8,128)(2,1)}, u32[]{:S(2)}) %copy-start.2) | copy-done | bytes 2097176
  3.9 0.0 copy-start.3
  3.9 1.0 %copy-done.3 = bf16[1024,256]{1,0:T(8,128)(2,1)S(1)} copy-done((bf16[1024,256]{1,0:T(8,128)(2,1)S(1)}, bf16[1024,256]{1,0:T(8,128)(2,1)}, u32[]{:S(2)}) %copy-start.3) | copy-done | bytes 524312
  4.9 0.0 copy-start
  4.9 52.2 %shard_map.55 = (bf16[8,2,128,1024]{3,2,1,0:T(8,128)(2,1)S(1)}, bf16[1024,1024]{1,0:T(8,128)(2,1)S(1)}) custom-call(s32[64]{0:T(128)S(1)} %copy-done.1, s32[24]{0:T(128)S(1)} %select_reduce_fusion.table_ref.table, bf16[8,128,256]{2,1,0:T(8,128)(2,1)S(1)} %bitcast.1, bf16[1024,1024]{1,0:T(8,128)(2,1)S(1)} %copy-done.2), custom_call_target="tpu_custom_call" | custom-call | flops 2684354560 | bytes 62914560 | tf_op jit(solution)/shard_map/pallas_call | solution.py:218
  57.1 0.0 copy-done
  57.1 8.4 %shard_map.56 = f32[2048,1024]{1,0:T(8,128)} custom-call(s32[24]{0:T(128)S(1)} %select_reduce_fusion.table_ref.table, s32[16,8]{1,0:T(8,128)S(1)} %copy.7.pat_ref, bf16[8,2,128,1024]{3,2,1,0:T(8,128)(2,1)S(1)} %get-tuple-element.7.low_ref.high_ref, bf16[8,2,128,1024]{3,2,1,0:T(8,128)(2,1)S(1)} %get-tuple-element.7.low_ref.high_ref, ...), custom_call_target="tpu_custom_call" | custom-call | tf_op jit(solution)/shard_map/pallas_call | solution.py:257
  (2 shorter events, 0.0 us)
Async XLA Ops:
  1.6 0.7 %copy-start.1 = (s32[64]{0:T(128)S(1)}, s32[64]{0:T(128)}, u32[]{:S(2)}) copy-start(s32[64]{0:T(128)} %perm_ref.1) | copy-start | bytes 772
  2.3 1.6 %copy-start.2 = (bf16[1024,1024]{1,0:T(8,128)(2,1)S(1)}, bf16[1024,1024]{1,0:T(8,128)(2,1)}, u32[]{:S(2)}) copy-start(bf16[1024,1024]{1,0:T(8,128)(2,1)} %d_hbm.1) | copy-start | bytes 6291460
  3.9 1.0 %copy-start.3 = (bf16[1024,256]{1,0:T(8,128)(2,1)S(1)}, bf16[1024,256]{1,0:T(8,128)(2,1)}, u32[]{:S(2)}) copy-start(bf16[1024,256]{1,0:T(8,128)(2,1)} %param.6) | copy-start | bytes 1572868
  4.9 52.2 %copy-start = (f32[2048,1024]{1,0:T(8,128)S(1)}, f32[2048,1024]{1,0:T(8,128)}, u32[]{:S(2)}) copy-start(f32[2048,1024]{1,0:T(8,128)} %schur_ref.1) | copy-start | bytes 25165828

commit v4 on v3

--- a/solution.py
+++ b/solution.py
@@ -18,8 +18,8 @@
 
 
 def exchange_kernel(
-    n_row, n_col, gpr, held, block_cols,
-    perm_ref, table_ref, raw_hbm, d_hbm, rows_ref, cols_ref,
+    n_row, n_col, gpr, held, block_cols, block_rows,
+    perm_ref, raw_hbm, d_hbm, rows_ref, cols_ref, table_ref,
     raw_ref, sorted_ref, a_ref, b_ref, own_ref, d_ref, cpan_ref,
     a_send, a_recv, b_send, b_recv, c_send, c_recv,
     up_send, up_recv, down_send, down_recv, f_send, f_recv, loc,
@@ -122,12 +122,25 @@
         c_copy(dr).start()
     cpan_ref[:, :, part(r)] = b_ref[...]
 
+    wanted = [c * block_cols + k for k in range(block_cols)]
+    wanted += [r * block_rows + k for k in range(block_rows)]
+
+    def look(p, found):
+        at, holder = perm_ref[p], p // held
+        return tuple(jnp.where(at == w, holder, f) for w, f in zip(wanted, found))
+
+    holders = lax.fori_loop(
+        0, perm_ref.shape[0], look, tuple(jnp.int32(0) for _ in wanted)
+    )
+    for k, value in enumerate(holders):
+        table_ref[k] = value
+
     def factor_columns():
         for dr in range(1, n_row):
             c_copy(dr, (r + n_row - dr) % n_row).wait_recv()
         step = 4 if block_cols % 4 == 0 else 1
         for w in range(0, block_cols, step):
-            left = jnp.concatenate([cpan_ref[table_ref[w + k]] for k in range(step)], axis=0)
+            left = jnp.concatenate([cpan_ref[holders[w + k]] for k in range(step)], axis=0)
             done = times_inverse(left, d_ref[...]).astype(jnp.bfloat16)
             cols_ref[w * BLK:(w + step) * BLK, :] = done
 
@@ -180,17 +193,16 @@
     keep.wait()
 
 
-def update_kernel(
-    table, pat_ref, low_ref, high_ref, cols_ref, schur_ref, out_ref,
-):
+def update_kernel(tile, table, pat_ref, *refs):
+    row_refs, (cols_ref, schur_ref, out_ref) = refs[:tile], refs[tile:]
     i = pl.program_id(0)
-    left = jnp.concatenate([low_ref[0, 0], high_ref[0, 0]], axis=0)
+    left = jnp.concatenate([ref[0, 0] for ref in row_refs], axis=0)
     update = times_inverse(left, cols_ref[...])
-    for e in range(2):
+    for e in range(tile):
         rows = slice(e * BLK, (e + 1) * BLK)
         for w in range(cols_ref.shape[0] // BLK):
             at = slice(w * BLK, (w + 1) * BLK)
-            weight = pat_ref[2 * i + e, w].astype(jnp.float32)
+            weight = pat_ref[w, tile * i + e].astype(jnp.float32)
             out_ref[rows, at] = schur_ref[rows, at] - update[rows, at] * weight
 
 
@@ -207,24 +219,22 @@
     blocks = perm.shape[0]
     bf16 = jnp.bfloat16
 
-    at = jnp.arange(block_cols + block_rows, dtype=jnp.int32)
-    ids = jnp.where(at < block_cols, c * block_cols + at, r * block_rows + at - block_cols)
-    holder = lax.div(lax.broadcasted_iota(jnp.int32, (ids.shape[0], blocks), 1), held)
-    table = jnp.sum(jnp.where(perm[None, :] == ids[:, None], holder, 0), axis=1)
     n_pos = n_col // 2
     dma = pltpu.SemaphoreType.DMA
     smem = pl.BlockSpec(memory_space=pltpu.SMEM)
     hbm = pl.BlockSpec(memory_space=pltpu.HBM)
-    rows, cols = pl.pallas_call(
-        functools.partial(exchange_kernel, n_row, n_col, gpr, held, block_cols),
+    rows, cols, table = pl.pallas_call(
+        functools.partial(exchange_kernel, n_row, n_col, gpr, held, block_cols, block_rows),
         out_shape=(
             jax.ShapeDtypeStruct((n_col, gpr, BLK, snw), bf16),
             jax.ShapeDtypeStruct((local_cols, snw), bf16),
-        ),
-        in_specs=[smem, smem, hbm, hbm],
+            jax.ShapeDtypeStruct((block_cols + block_rows,), jnp.int32),
+        ),
+        in_specs=[smem, hbm, hbm],
         out_specs=(
             pl.BlockSpec(memory_space=pl.ANY),
             pl.BlockSpec(memory_space=pltpu.VMEM),
+            smem,
         ),
         scratch_shapes=[
             pltpu.VMEM((held, BLK, kw), bf16),
@@ -246,30 +256,29 @@
             bytes_accessed=30 * local_rows * snw,
             transcendentals=0,
         ),
-    )(perm, table, panel_raw.reshape(held, BLK, kw), diag_inverse)
+    )(perm, panel_raw.reshape(held, BLK, kw), diag_inverse)
+
+    tile = 4 if block_rows % 4 == 0 else 1
 
     def row_spec(e):
         return pl.BlockSpec(
             (1, 1, BLK, snw),
-            lambda i, t, p: (t[block_cols + 2 * i + e], (2 * i + e) // block_cols, 0, 0),
+            lambda i, t, p: (t[block_cols + tile * i + e], (tile * i + e) // block_cols, 0, 0),
         )
 
+    wide = pl.BlockSpec((tile * BLK, local_cols), lambda i, t, p: (i, 0))
     return pl.pallas_call(
-        update_kernel,
+        functools.partial(update_kernel, tile),
         out_shape=jax.ShapeDtypeStruct(schur.shape, schur.dtype),
         grid_spec=pltpu.PrefetchScalarGridSpec(
             num_scalar_prefetch=2,
-            grid=(block_rows // 2,),
-            in_specs=[
-                row_spec(0),
-                row_spec(1),
-                pl.BlockSpec((local_cols, snw), lambda i, t, p: (0, 0)),
-                pl.BlockSpec((2 * BLK, local_cols), lambda i, t, p: (i, 0)),
-            ],
-            out_specs=pl.BlockSpec((2 * BLK, local_cols), lambda i, t, p: (i, 0)),
-        ),
-        compiler_params=pltpu.CompilerParams(vmem_limit_bytes=20 * 2**20),
-    )(table, pattern, rows, rows, cols, schur)
+            grid=(block_rows // tile,),
+            in_specs=[row_spec(e) for e in range(tile)]
+            + [pl.BlockSpec((local_cols, snw), lambda i, t, p: (0, 0)), wide],
+            out_specs=wide,
+        ),
+        compiler_params=pltpu.CompilerParams(vmem_limit_bytes=28 * 2**20),
+    )(table, pattern.T, *([rows] * tile), cols, schur)
 
 
 def solution(mesh):

time: 65.7 us -> 63.4 us (0.965)
  other arithmetic: 0.84 us -> 0 us
  local copies, waits for them, and re-layouts: 4.05 us -> 3.29 us
    pallas_call x1, Pallas kernels: 8.37 us -> 7.16 us  [local(): pl.pallas_call(functools.partial(update_kernel, tile), out_shape=jax.Shap...]
    reduce_sum x1 -> x0, other arithmetic: 0.83 us -> none  [local(): table = jnp.sum(jnp.where(perm[None, :] == ids[:, None], holder, 0), axis=1)]
    unnamed x9 -> x10, local copies, waits for them, and re-layouts: 4.05 us -> 3.29 us
where the time goes in v4:
time: 63.4 us; the launch traced here: 63.2 us
  Pallas kernels  59.9 us (94%)
  local copies, waits for them, and re-layouts  3.29 us (5%)
    pallas_call x1, Pallas kernels, local(): pl.pallas_call(functools.partial(exchange_kernel, n_row, n_col, gpr, held...  52.7 us
    pallas_call x1, Pallas kernels, local(): pl.pallas_call(functools.partial(update_kernel, tile), out_shape=jax.Shap...  7.16 us
    unnamed x10, local copies, waits for them, and re-layouts  3.29 us

profile of v4, /device:TPU:0, one launch (start us, length us, event | category | flops | bytes accessed | tf_op | source)
XLA Modules:
  0.0 63.2 jit_solution(9973007708594641466)
XLA Ops:
  0.0 0.0 copy-start.2
  0.0 1.6 %copy-done.2 = bf16[1024,1024]{1,0:T(8,128)(2,1)S(1)} copy-done((bf16[1024,1024]{1,0:T(8,128)(2,1)S(1)}, bf16[1024,1024]{1,0:T(8,128)(2,1)}, u32[]{:S(2)}) %copy-start.2) | copy-done | bytes 2097176
  1.6 0.0 copy-start.3
  1.6 1.0 %copy-done.3 = bf16[1024,256]{1,0:T(8,128)(2,1)S(1)} copy-done((bf16[1024,256]{1,0:T(8,128)(2,1)S(1)}, bf16[1024,256]{1,0:T(8,128)(2,1)}, u32[]{:S(2)}) %copy-start.3) | copy-done | bytes 524312
  2.6 0.0 copy-start.4
  2.6 0.7 %copy-done.4 = s32[64]{0:T(128)S(1)} copy-done((s32[64]{0:T(128)S(1)}, s32[64]{0:T(128)}, u32[]{:S(2)}) %copy-start.4) | copy-done | bytes 280
  3.3 0.0 copy-start
  3.3 0.0 copy-start.1
  3.3 52.7 %shard_map.55 = (bf16[8,2,128,1024]{3,2,1,0:T(8,128)(2,1)S(1)}, bf16[1024,1024]{1,0:T(8,128)(2,1)S(1)}, s32[24]{0:T(128)S(1)}) custom-call(s32[64]{0:T(128)S(1)} %copy-done.4, bf16[8,128,256]{2,1,0:T(8,128)(2,1)S(1)} %bitcast.3, bf16[1024,1024]{1,0:T(8,128)(2,1)S(1)} %copy-done.2), custom_call_target="tpu_custom_call" | custom-call | flops 2684354560 | bytes 62914560 | tf_op jit(solution)/shard_map/pallas_call | solution.py:226
  56.0 0.0 copy-done
  56.1 0.0 copy-done.1
  56.1 7.2 %shard_map.56 = f32[2048,1024]{1,0:T(8,128)} custom-call(s32[24]{0:T(128)S(1)} %get-tuple-element.8.table, s32[8,16]{1,0:T(8,128)S(1)} %bitcast.2, bf16[8,2,128,1024]{3,2,1,0:T(8,128)(2,1)S(1)} %get-tuple-element.9.refs_0_.refs_1_.refs_2_.refs_3_, bf16[8,2,128,1024]{3,2,1,0:T(8,128)(2,1)S(1)} %get-tuple-element.9.refs_0_.refs_1_.refs_2_.refs_3_, ...), custom_call_target="tpu_custom_call" | custom-call | tf_op jit(solution)/shard_map/pallas_call | solution.py:270
Async XLA Ops:
  0.0 1.6 %copy-start.2 = (bf16[1024,1024]{1,0:T(8,128)(2,1)S(1)}, bf16[1024,1024]{1,0:T(8,128)(2,1)}, u32[]{:S(2)}) copy-start(bf16[1024,1024]{1,0:T(8,128)(2,1)} %d_hbm.1) | copy-start | bytes 6291460
  1.6 1.0 %copy-start.3 = (bf16[1024,256]{1,0:T(8,128)(2,1)S(1)}, bf16[1024,256]{1,0:T(8,128)(2,1)}, u32[]{:S(2)}) copy-start(bf16[1024,256]{1,0:T(8,128)(2,1)} %param.6) | copy-start | bytes 1572868
  2.6 0.7 %copy-start.4 = (s32[64]{0:T(128)S(1)}, s32[64]{0:T(128)}, u32[]{:S(2)}) copy-start(s32[64]{0:T(128)} %perm_ref.1) | copy-start | bytes 772
  3.3 52.8 %copy-start = (f32[2048,1024]{1,0:T(8,128)S(1)}, f32[2048,1024]{1,0:T(8,128)}, u32[]{:S(2)}) copy-start(f32[2048,1024]{1,0:T(8,128)} %refs_5_.1) | copy-start | bytes 25165828
  3.3 52.8 %copy-start.1 = (s32[16,8]{0,1:T(8,128)S(1)}, s32[16,8]{0,1:T(8,128)}, u32[]{:S(2)}) copy-start(s32[16,8]{0,1:T(8,128)} %param.9) | copy-start | bytes 1540

commit v5 on v4

--- a/solution.py
+++ b/solution.py
@@ -19,8 +19,8 @@
 
 def exchange_kernel(
     n_row, n_col, gpr, held, block_cols, block_rows,
-    perm_ref, raw_hbm, d_hbm, rows_ref, cols_ref, table_ref,
-    raw_ref, sorted_ref, a_ref, b_ref, own_ref, d_ref, cpan_ref,
+    perm_ref, raw_hbm, d_hbm, rows_ref, cols_hbm, table_ref,
+    raw_ref, sorted_ref, a_ref, b_ref, own_ref, d_ref, cpan_ref, cols_ref,
     a_send, a_recv, b_send, b_recv, c_send, c_recv,
     up_send, up_recv, down_send, down_recv, f_send, f_recv, loc,
 ):
@@ -60,26 +60,25 @@
         sorted_ref[g] = raw_ref[block]
     pl.semaphore_wait(barrier, n_row + n_col - 2)
 
-    def a_copy(dr, came=None):
+    def a_copy(dr, q, came=None):
         to = (r + dr) % n_row
-        return remote(sorted_ref.at[pl.ds(to * gpr, gpr)],
-                      a_ref.at[:, :, part(r if came is None else came)],
-                      a_send.at[dr], a_recv.at[dr], to, c)
+        return remote(sorted_ref.at[to * gpr + q],
+                      a_ref.at[q, :, part(r if came is None else came)],
+                      a_send.at[dr, q], a_recv.at[dr, q], to, c)
 
     def b_copy(dc, came=None):
         to = (c + dc) % n_col
         return remote(sorted_ref.at[to], b_ref.at[c if came is None else came],
                       b_send.at[dc], b_recv.at[dc], r, to)
 
-    for dr in range(1, n_row):
-        a_copy(dr).start()
+    for q in range(gpr):
+        for dr in range(1, n_row):
+            a_copy(dr, q).start()
     for dc in range(1, n_col):
         b_copy(dc).start()
     a_ref[:, :, part(r)] = sorted_ref[pl.ds(r * gpr, gpr)]
     b_ref[c] = sorted_ref[c]
     load_d.wait()
-    for dr in range(1, n_row):
-        a_copy(dr, (r + n_row - dr) % n_row).wait_recv()
     def up_copy(d, q):
         slot = (pos - d) * 2 + core
         return remote(own_ref.at[q] if d == 0 else rows_ref.at[slot, q], rows_ref.at[slot, q],
@@ -96,6 +95,8 @@
                       f_send.at[source, q], f_recv.at[source, q], r, sibling)
 
     for q in range(gpr):
+        for dr in range(1, n_row):
+            a_copy(dr, q, (r + n_row - dr) % n_row).wait_recv()
         own_ref[q] = times_inverse(a_ref[q], d_ref[...]).astype(jnp.bfloat16)
 
         @pl.when(pos < n_pos - 1)
@@ -134,6 +135,8 @@
     )
     for k, value in enumerate(holders):
         table_ref[k] = value
+
+    keep_cols = pltpu.make_async_copy(cols_ref, cols_hbm, loc.at[2])
 
     def factor_columns():
         for dr in range(1, n_row):
@@ -143,6 +146,7 @@
             left = jnp.concatenate([cpan_ref[holders[w + k]] for k in range(step)], axis=0)
             done = times_inverse(left, d_ref[...]).astype(jnp.bfloat16)
             cols_ref[w * BLK:(w + step) * BLK, :] = done
+        keep_cols.start()
 
     for d in range(1, n_pos):
         if d == n_pos - 1:
@@ -172,7 +176,8 @@
                 side_copy(pos + d, q, False).start()
 
     for dr in range(1, n_row):
-        a_copy(dr).wait_send()
+        for q in range(gpr):
+            a_copy(dr, q).wait_send()
         c_copy(dr).wait_send()
     for dc in range(1, n_col):
         b_copy(dc).wait_send()
@@ -191,6 +196,7 @@
                    f_recv.at[source, q], r, sibling).wait_recv()
             side_copy(source, q, True).wait_send()
     keep.wait()
+    keep_cols.wait()
 
 
 def update_kernel(tile, table, pat_ref, *refs):
@@ -233,7 +239,7 @@
         in_specs=[smem, hbm, hbm],
         out_specs=(
             pl.BlockSpec(memory_space=pl.ANY),
-            pl.BlockSpec(memory_space=pltpu.VMEM),
+            pl.BlockSpec(memory_space=pl.ANY),
             smem,
         ),
         scratch_shapes=[
@@ -244,12 +250,13 @@
             pltpu.VMEM((gpr, BLK, snw), bf16),
             pltpu.VMEM((snw, snw), bf16),
             pltpu.VMEM((n_col, BLK, snw), bf16),
-            dma((n_row,)), dma((n_row,)), dma((n_col,)), dma((n_col,)),
+            pltpu.VMEM((local_cols, snw), bf16),
+            dma((n_row, gpr)), dma((n_row, gpr)), dma((n_col,)), dma((n_col,)),
             dma((n_row,)), dma((n_row,)), dma((n_pos, gpr)), dma((n_pos, gpr)),
             dma((n_pos, gpr)), dma((n_pos, gpr)), dma((n_pos, gpr)), dma((n_pos, gpr)), dma((4,)),
         ],
         compiler_params=pltpu.CompilerParams(
-            collective_id=0, has_side_effects=True, vmem_limit_bytes=20 * 2**20
+            collective_id=0, has_side_effects=True, vmem_limit_bytes=58 * 2**20
         ),
         cost_estimate=pl.CostEstimate(
             flops=2 * (local_cols + gpr * BLK) * snw * snw,
@@ -277,7 +284,7 @@
             + [pl.BlockSpec((local_cols, snw), lambda i, t, p: (0, 0)), wide],
             out_specs=wide,
         ),
-        compiler_params=pltpu.CompilerParams(vmem_limit_bytes=28 * 2**20),
+        compiler_params=pltpu.CompilerParams(vmem_limit_bytes=58 * 2**20),
     )(table, pattern.T, *([rows] * tile), cols, schur)
 
 

time: 63.4 us -> 64.9 us (1.024)
  Pallas kernels: 59.9 us -> 64.7 us
  local copies, waits for them, and re-layouts: 3.29 us -> 0 us
    pallas_call x1, Pallas kernels: 7.16 us -> 12.2 us  [local(): pl.pallas_call(functools.partial(update_kernel, tile), out_shape=jax.Shap...]
    unnamed x10 -> x0, local copies, waits for them, and re-layouts: 3.29 us -> none
where the time goes in v5:
time: 64.9 us; the launch traced here: 64.7 us
  Pallas kernels  64.7 us (100%)
    pallas_call x1, Pallas kernels, local(): pl.pallas_call(functools.partial(exchange_kernel, n_row, n_col, gpr, held...  52.5 us
    pallas_call x1, Pallas kernels, local(): pl.pallas_call(functools.partial(update_kernel, tile), out_shape=jax.Shap...  12.2 us

profile of v5, /device:TPU:0, one launch (start us, length us, event | category | flops | bytes accessed | tf_op | source)
XLA Modules:
  0.0 64.7 jit_solution(7081197841999928753)
XLA Ops:
  0.0 52.5 %shard_map.55 = (bf16[8,2,128,1024]{3,2,1,0:T(8,128)(2,1)}, bf16[1024,1024]{1,0:T(8,128)(2,1)}, s32[24]{0:T(128)}) custom-call(s32[64]{0:T(128)} %perm_ref.1, bf16[8,128,256]{2,1,0:T(8,128)(2,1)} %bitcast.3, bf16[1024,1024]{1,0:T(8,128)(2,1)} %d_hbm.1), custom_call_target="tpu_custom_call" | custom-call | flops 2684354560 | bytes 62914560 | tf_op jit(solution)/shard_map/pallas_call | solution.py:232
  52.5 12.2 %shard_map.56 = f32[2048,1024]{1,0:T(8,128)} custom-call(s32[24]{0:T(128)} %get-tuple-element.8.table, s32[8,16]{1,0:T(8,128)} %bitcast.2, bf16[8,2,128,1024]{3,2,1,0:T(8,128)(2,1)} %get-tuple-element.9.refs_0_.refs_1_.refs_2_.refs_3_, bf16[8,2,128,1024]{3,2,1,0:T(8,128)(2,1)} %get-tuple-element.9.refs_0_.refs_1_.refs_2_.refs_3_, ...), custom_call_target="tpu_custom_call" | custom-call | tf_op jit(solution)/shard_map/pallas_call | solution.py:277

commit v6 on v5

--- a/solution.py
+++ b/solution.py
@@ -256,7 +256,7 @@
             dma((n_pos, gpr)), dma((n_pos, gpr)), dma((n_pos, gpr)), dma((n_pos, gpr)), dma((4,)),
         ],
         compiler_params=pltpu.CompilerParams(
-            collective_id=0, has_side_effects=True, vmem_limit_bytes=58 * 2**20
+            collective_id=0, has_side_effects=True, vmem_limit_bytes=20 * 2**20
         ),
         cost_estimate=pl.CostEstimate(
             flops=2 * (local_cols + gpr * BLK) * snw * snw,
@@ -284,7 +284,7 @@
             + [pl.BlockSpec((local_cols, snw), lambda i, t, p: (0, 0)), wide],
             out_specs=wide,
         ),
-        compiler_params=pltpu.CompilerParams(vmem_limit_bytes=58 * 2**20),
+        compiler_params=pltpu.CompilerParams(vmem_limit_bytes=28 * 2**20),
     )(table, pattern.T, *([rows] * tile), cols, schur)
 
 

time: 64.9 us -> 62.8 us (0.968)
  Pallas kernels: 64.7 us -> 59.3 us
  local copies, waits for them, and re-layouts: 0 us -> 3.29 us
    pallas_call x1, Pallas kernels: 12.2 us -> 7.16 us  [local(): pl.pallas_call(functools.partial(update_kernel, tile), out_shape=jax.Shap...]
    unnamed x0 -> x10, local copies, waits for them, and re-layouts: none -> 3.29 us
where the time goes in v6:
time: 62.8 us; the launch traced here: 62.6 us
  Pallas kernels  59.3 us (94%)
  local copies, waits for them, and re-layouts  3.29 us (5%)
    pallas_call x1, Pallas kernels, local(): pl.pallas_call(functools.partial(exchange_kernel, n_row, n_col, gpr, held...  52.1 us
    pallas_call x1, Pallas kernels, local(): pl.pallas_call(functools.partial(update_kernel, tile), out_shape=jax.Shap...  7.16 us
    unnamed x10, local copies, waits for them, and re-layouts  3.29 us

profile of v6, /device:TPU:0, one launch (start us, length us, event | category | flops | bytes accessed | tf_op | source)
XLA Modules:
  0.0 62.6 jit_solution(14568051592575014833)
XLA Ops:
  0.0 0.0 copy-start.2
  0.0 1.6 %copy-done.2 = bf16[1024,1024]{1,0:T(8,128)(2,1)S(1)} copy-done((bf16[1024,1024]{1,0:T(8,128)(2,1)S(1)}, bf16[1024,1024]{1,0:T(8,128)(2,1)}, u32[]{:S(2)}) %copy-start.2) | copy-done | bytes 2097176
  1.6 0.0 copy-start.3
  1.6 1.0 %copy-done.3 = bf16[1024,256]{1,0:T(8,128)(2,1)S(1)} copy-done((bf16[1024,256]{1,0:T(8,128)(2,1)S(1)}, bf16[1024,256]{1,0:T(8,128)(2,1)}, u32[]{:S(2)}) %copy-start.3) | copy-done | bytes 524312
  2.6 0.0 copy-start.4
  2.6 0.7 %copy-done.4 = s32[64]{0:T(128)S(1)} copy-done((s32[64]{0:T(128)S(1)}, s32[64]{0:T(128)}, u32[]{:S(2)}) %copy-start.4) | copy-done | bytes 280
  3.3 0.0 copy-start
  3.3 0.0 copy-start.1
  3.3 52.1 %shard_map.55 = (bf16[8,2,128,1024]{3,2,1,0:T(8,128)(2,1)S(1)}, bf16[1024,1024]{1,0:T(8,128)(2,1)S(1)}, s32[24]{0:T(128)S(1)}) custom-call(s32[64]{0:T(128)S(1)} %copy-done.4, bf16[8,128,256]{2,1,0:T(8,128)(2,1)S(1)} %bitcast.3, bf16[1024,1024]{1,0:T(8,128)(2,1)S(1)} %copy-done.2), custom_call_target="tpu_custom_call" | custom-call | flops 2684354560 | bytes 62914560 | tf_op jit(solution)/shard_map/pallas_call | solution.py:232
  55.4 0.0 copy-done
  55.5 0.0 copy-done.1
  55.5 7.2 %shard_map.56 = f32[2048,1024]{1,0:T(8,128)} custom-call(s32[24]{0:T(128)S(1)} %get-tuple-element.8.table, s32[8,16]{1,0:T(8,128)S(1)} %bitcast.2, bf16[8,2,128,1024]{3,2,1,0:T(8,128)(2,1)S(1)} %get-tuple-element.9.refs_0_.refs_1_.refs_2_.refs_3_, bf16[8,2,128,1024]{3,2,1,0:T(8,128)(2,1)S(1)} %get-tuple-element.9.refs_0_.refs_1_.refs_2_.refs_3_, ...), custom_call_target="tpu_custom_call" | custom-call | tf_op jit(solution)/shard_map/pallas_call | solution.py:277
Async XLA Ops:
  0.0 1.6 %copy-start.2 = (bf16[1024,1024]{1,0:T(8,128)(2,1)S(1)}, bf16[1024,1024]{1,0:T(8,128)(2,1)}, u32[]{:S(2)}) copy-start(bf16[1024,1024]{1,0:T(8,128)(2,1)} %d_hbm.1) | copy-start | bytes 6291460
  1.6 1.0 %copy-start.3 = (bf16[1024,256]{1,0:T(8,128)(2,1)S(1)}, bf16[1024,256]{1,0:T(8,128)(2,1)}, u32[]{:S(2)}) copy-start(bf16[1024,256]{1,0:T(8,128)(2,1)} %param.6) | copy-start | bytes 1572868
  2.6 0.7 %copy-start.4 = (s32[64]{0:T(128)S(1)}, s32[64]{0:T(128)}, u32[]{:S(2)}) copy-start(s32[64]{0:T(128)} %perm_ref.1) | copy-start | bytes 772
  3.3 52.2 %copy-start = (f32[2048,1024]{1,0:T(8,128)S(1)}, f32[2048,1024]{1,0:T(8,128)}, u32[]{:S(2)}) copy-start(f32[2048,1024]{1,0:T(8,128)} %refs_5_.1) | copy-start | bytes 25165828
  3.3 52.2 %copy-start.1 = (s32[16,8]{0,1:T(8,128)S(1)}, s32[16,8]{0,1:T(8,128)}, u32[]{:S(2)}) copy-start(s32[16,8]{0,1:T(8,128)} %param.9) | copy-start | bytes 1540

commit v7 on v6

--- a/solution.py
+++ b/solution.py
@@ -15,6 +15,16 @@
     return lax.dot_general(
         left, right, (((1,), (1,)), ((), ())), preferred_element_type=jnp.float32
     )
+
+
+def factor(left, d_ref):
+    size = d_ref.shape[0]
+    step = min(256, size)
+    parts = [
+        times_inverse(left[:, :k + step], d_ref[k:k + step, :k + step])
+        for k in range(0, size, step)
+    ]
+    return jnp.concatenate(parts, axis=1).astype(jnp.bfloat16)
 
 
 def exchange_kernel(
@@ -97,7 +107,7 @@
     for q in range(gpr):
         for dr in range(1, n_row):
             a_copy(dr, q, (r + n_row - dr) % n_row).wait_recv()
-        own_ref[q] = times_inverse(a_ref[q], d_ref[...]).astype(jnp.bfloat16)
+        own_ref[q] = factor(a_ref[q], d_ref)
 
         @pl.when(pos < n_pos - 1)
         def _(q=q):
@@ -144,7 +154,7 @@
         step = 4 if block_cols % 4 == 0 else 1
         for w in range(0, block_cols, step):
             left = jnp.concatenate([cpan_ref[holders[w + k]] for k in range(step)], axis=0)
-            done = times_inverse(left, d_ref[...]).astype(jnp.bfloat16)
+            done = factor(left, d_ref)
             cols_ref[w * BLK:(w + step) * BLK, :] = done
         keep_cols.start()
 

time: 62.8 us -> 62.8 us (level)
  no operation moved by 1% of the time
where the time goes in v7:
time: 62.8 us; the launch traced here: 62.6 us
  Pallas kernels  59.3 us (94%)
  local copies, waits for them, and re-layouts  3.29 us (5%)
    pallas_call x1, Pallas kernels, local(): pl.pallas_call(functools.partial(exchange_kernel, n_row, n_col, gpr, held...  52.1 us
    pallas_call x1, Pallas kernels, local(): pl.pallas_call(functools.partial(update_kernel, tile), out_shape=jax.Shap...  7.16 us
    unnamed x10, local copies, waits for them, and re-layouts  3.29 us

profile of v7, /device:TPU:0, one launch (start us, length us, event | category | flops | bytes accessed | tf_op | source)
XLA Modules:
  0.0 62.6 jit_solution(2733203773542405539)
XLA Ops:
  0.0 0.0 copy-start.2
  0.0 1.6 %copy-done.2 = bf16[1024,1024]{1,0:T(8,128)(2,1)S(1)} copy-done((bf16[1024,1024]{1,0:T(8,128)(2,1)S(1)}, bf16[1024,1024]{1,0:T(8,128)(2,1)}, u32[]{:S(2)}) %copy-start.2) | copy-done | bytes 2097176
  1.6 0.0 copy-start.3
  1.6 1.0 %copy-done.3 = bf16[1024,256]{1,0:T(8,128)(2,1)S(1)} copy-done((bf16[1024,256]{1,0:T(8,128)(2,1)S(1)}, bf16[1024,256]{1,0:T(8,128)(2,1)}, u32[]{:S(2)}) %copy-start.3) | copy-done | bytes 524312
  2.6 0.0 copy-start.4
  2.6 0.7 %copy-done.4 = s32[64]{0:T(128)S(1)} copy-done((s32[64]{0:T(128)S(1)}, s32[64]{0:T(128)}, u32[]{:S(2)}) %copy-start.4) | copy-done | bytes 280
  3.3 0.0 copy-start
  3.3 0.0 copy-start.1
  3.3 52.1 %shard_map.55 = (bf16[8,2,128,1024]{3,2,1,0:T(8,128)(2,1)S(1)}, bf16[1024,1024]{1,0:T(8,128)(2,1)S(1)}, s32[24]{0:T(128)S(1)}) custom-call(s32[64]{0:T(128)S(1)} %copy-done.4, bf16[8,128,256]{2,1,0:T(8,128)(2,1)S(1)} %bitcast.3, bf16[1024,1024]{1,0:T(8,128)(2,1)S(1)} %copy-done.2), custom_call_target="tpu_custom_call" | custom-call | flops 2684354560 | bytes 62914560 | tf_op jit(solution)/shard_map/pallas_call | solution.py:242
  55.4 0.0 copy-done
  55.5 0.0 copy-done.1
  55.5 7.2 %shard_map.56 = f32[2048,1024]{1,0:T(8,128)} custom-call(s32[24]{0:T(128)S(1)} %get-tuple-element.8.table, s32[8,16]{1,0:T(8,128)S(1)} %bitcast.2, bf16[8,2,128,1024]{3,2,1,0:T(8,128)(2,1)S(1)} %get-tuple-element.9.refs_0_.refs_1_.refs_2_.refs_3_, bf16[8,2,128,1024]{3,2,1,0:T(8,128)(2,1)S(1)} %get-tuple-element.9.refs_0_.refs_1_.refs_2_.refs_3_, ...), custom_call_target="tpu_custom_call" | custom-call | tf_op jit(solution)/shard_map/pallas_call | solution.py:287
Async XLA Ops:
  0.0 1.6 %copy-start.2 = (bf16[1024,1024]{1,0:T(8,128)(2,1)S(1)}, bf16[1024,1024]{1,0:T(8,128)(2,1)}, u32[]{:S(2)}) copy-start(bf16[1024,1024]{1,0:T(8,128)(2,1)} %d_hbm.1) | copy-start | bytes 6291460
  1.6 1.0 %copy-start.3 = (bf16[1024,256]{1,0:T(8,128)(2,1)S(1)}, bf16[1024,256]{1,0:T(8,128)(2,1)}, u32[]{:S(2)}) copy-start(bf16[1024,256]{1,0:T(8,128)(2,1)} %param.6) | copy-start | bytes 1572868
  2.6 0.7 %copy-start.4 = (s32[64]{0:T(128)S(1)}, s32[64]{0:T(128)}, u32[]{:S(2)}) copy-start(s32[64]{0:T(128)} %perm_ref.1) | copy-start | bytes 772
  3.3 52.2 %copy-start = (f32[2048,1024]{1,0:T(8,128)S(1)}, f32[2048,1024]{1,0:T(8,128)}, u32[]{:S(2)}) copy-start(f32[2048,1024]{1,0:T(8,128)} %refs_5_.1) | copy-start | bytes 25165828
  3.3 52.2 %copy-start.1 = (s32[16,8]{0,1:T(8,128)S(1)}, s32[16,8]{0,1:T(8,128)}, u32[]{:S(2)}) copy-start(s32[16,8]{0,1:T(8,128)} %param.9) | copy-start | bytes 1540
